TPU v7x, 128 devices: a whole 4x4x4 slice. The times are simulated.
128 devices in a mesh: dp: 8 (over z, x_hi), expert: 16 (over y, x_lo, core).
Axes of the slice: x: 4 (x_hi: 2, x_lo: 2; x = x_hi * 2 + x_lo), y: 4, z: 4, core: 2. Of those that a mesh axis runs over, the one named last changes fastest.
Arguments:
- activations: bfloat16 [16, 8192, 2048], P('expert', 'dp'), may hold values from -6 to 6
- grad_hidden: bfloat16 [16, 8192, 1536], P('expert', 'dp'), may hold values from -6 to 6
- counts: int32 [16, 8], P('expert', 'dp'), may hold values from 1 to 1024, as said below
- master: float32 [16, 2048, 1536], P('expert', 'dp'), may hold values from -0.125 to 0.125
- moment1: float32 [16, 2048, 1536], P('expert', 'dp'), may hold values from -3 to 3
- moment2: float32 [16, 2048, 1536], P('expert', 'dp'), may hold values from 0.01 to 1
- old_slot: int32 [16], replicated, may hold values from 0 to 15, each once
- new_slot: int32 [16], replicated, may hold values from 0 to 15, each once
Outputs:
- master_out: float32 [16, 2048, 1536], P('expert', 'dp')
- moment1_out: float32 [16, 2048, 1536], P('expert', 'dp')
- moment2_out: float32 [16, 2048, 1536], P('expert', 'dp')
- new_weight: bfloat16 [16, 2048, 1536], P('expert')
Inputs may be any that keep to these rules, and one draw needn't show every extreme that they name: `counts`: each entry is at most 1024, and some entry equals 1024.
All inputs are finite; a program needn't handle non-finite values.
Results may differ from a plain program's by a relative error of at most 0.0055.
Values may be sent and summed in bfloat16 or wider, within the bound.
A program may use at most 128 MiB of HBM per device.

v0:
```python
import math
import jax
import jax.numpy as jnp
from jax import lax
from jax.sharding import Mesh
from jax.sharding import PartitionSpec as P

EXPERT = ("expert_0", "expert_1", "expert_2")
beta_one = 0.9
beta_two = 0.95
learn_rate = 0.01
decay_rate = 0.1
adam_eps = 1e-08
step_number = 20


def in_blocks(value, dim, peers):
    dims = value.shape
    blocks = value.reshape(*dims[:dim], peers, dims[dim] // peers, *dims[dim + 1 :])
    return jnp.moveaxis(blocks, dim, 0)


def sent_and_summed(value, axis, dim):
    blocks = in_blocks(value, dim, lax.axis_size(axis))
    arrived = lax.all_to_all(blocks, axis, split_axis=0, concat_axis=0, tiled=True)
    return arrived.astype(jnp.float32).sum(axis=0)


def in_order(blocks, dim):
    blocks = jnp.moveaxis(blocks, 0, dim)
    dims = blocks.shape
    return blocks.reshape(*dims[:dim], dims[dim] * dims[dim + 1], *dims[dim + 2 :])


def exchange_in_order(blocks, axes, sequence):
    inside = blocks.shape[1:]
    whole = blocks.reshape(*(lax.axis_size(a) for a in axes), *inside)
    for k in sequence:
        whole = lax.all_to_all(whole, axes[k], k, k, tiled=True)
    return whole.reshape(-1, *inside)


def core_and_chips(value, groups, sequence, split_dim, concat_dim):
    peers = lax.axis_size(groups[0]) * lax.axis_size(groups[1])
    blocks = in_blocks(value, split_dim, peers)
    return in_order(exchange_in_order(blocks, groups, sequence), concat_dim)


def source_slots(old_slot, new_slot):
    slots = old_slot.shape[0]
    wanted = jnp.arange(slots, dtype=jnp.int32)
    picked = jnp.where(new_slot[None, :] == wanted[:, None], old_slot[None, :], 0)
    return jnp.sum(picked, axis=1)


def adamw(grads, master, moment1, moment2):
    first = beta_one * moment1 + (1.0 - beta_one) * grads
    second = beta_two * moment2 + (1.0 - beta_two) * grads * grads
    first_hat = first / (1.0 - beta_one**step_number)
    second_hat = second / (1.0 - beta_two**step_number)
    updated = master - learn_rate * (
        first_hat / (jnp.sqrt(second_hat) + adam_eps) + decay_rate * master
    )
    return (updated, first, second)


def on_device(activations, grad_hidden, counts, master, moment1, moment2, old_slot, new_slot):
    tokens_here = activations.shape[1]
    inputs = activations[0]
    row_index = jnp.arange(tokens_here, dtype=jnp.int32)
    cotangent = jnp.where(
        (row_index < counts[0, 0])[:, None], grad_hidden[0], jnp.zeros((), jnp.bfloat16)
    )
    grad_scale = 1.0 / math.sqrt(tokens_here * lax.axis_size("dp"))
    product = lax.dot_general(
        inputs, cotangent, (((0,), (0,)), ((), ())), preferred_element_type=jnp.float32
    )
    grads = sent_and_summed((product * grad_scale).astype(jnp.bfloat16), "dp", 0)
    updated, first, second = adamw(grads, master[0], moment1[0], moment2[0])
    weight_half = updated.astype(jnp.bfloat16)[None]
    source = source_slots(old_slot, new_slot)
    spread = core_and_chips(weight_half, (("expert_0", "expert_1"), "expert_2"), (1, 0), 1, 0)
    placed = lax.all_to_all(
        jnp.take(spread, source, axis=0), EXPERT, split_axis=0, concat_axis=1, tiled=True
    )
    moved = lax.all_gather(placed, "dp", axis=1, tiled=True)
    return (updated[None], first[None], second[None], moved)


def solution(mesh):
    finer = Mesh(
        mesh.devices.reshape(mesh.shape["dp"], 4, 2, 2), ("dp", "expert_0", "expert_1", "expert_2")
    )
    in_specs = (
        P(EXPERT, "dp", None),
        P(EXPERT, "dp", None),
        P(EXPERT, "dp"),
        P(EXPERT, "dp", None),
        P(EXPERT, "dp", None),
        P(EXPERT, "dp", None),
        P(),
        P(),
    )
    out_specs = (
        P(EXPERT, "dp", None),
        P(EXPERT, "dp", None),
        P(EXPERT, "dp", None),
        P(EXPERT, None, None),
    )
    return jax.shard_map(
        on_device, mesh=finer, in_specs=in_specs, out_specs=out_specs, check_vma=False
    )
```

profile of v0, /device:TPU:0, one launch (start us, length us, event | category | flops | bytes accessed | tf_op | source)
XLA Modules:
  0.0 260.9 jit_solution(13356812411573862050)
XLA Ops:
  7.8 9.9 %multiply_convert_fusion = bf16[1536,2048]{1,0:T(8,128)(2,1)S(1)} fusion(bf16[1,1024,2048]{2,1,0:T(8,128)(2,1)} %param.8, bf16[1,1024,1536]{2,1,0:T(8,128)(2,1)} %param.9, pred[1024]{0:T(1024)(128)(4,1)S(1)} %iota_compare_fusion.1), kind=kOutput, calls=%fused_computation.2 | convolution fusion | flops 6450315264 | bytes 13632512 | tf_op jit(solution)/shard_map/dot_general | solution.py:75
  17.7 3.1 %copy.58 = bf16[192,8,8,256]{3,2,0,1:T(8,128)(2,1)} copy(bf16[192,8,8,256]{3,2,1,0:T(8,128)(2,1)S(1)} %bitcast.31) | data formatting | bytes 12582912 | tf_op jit(solution)/shard_map/reshape | solution.py:19
  20.8 0.0 copy-start
  20.8 8.0 %all-to-all-start = ((bf16[8,256,1536]{1,2,0:T(8,128)(2,1)}), bf16[8,256,1536]{1,2,0:T(8,128)(2,1)}, u32[]{:S(2)}, u32[]{:S(2)}) async-start(bf16[8,256,1536]{1,2,0:T(8,128)(2,1)} %bitcast.30), calls=%async_computation | async-start | bytes 12582912 | tf_op jit(solution)/shard_map/all_to_all | solution.py:25
  28.8 0.0 copy-done
  28.8 0.0 copy-start.5
  28.8 1.6 copy.46
  30.4 0.0 copy-done.5
  30.4 1.6 copy.41
  32.1 3.0 %copy.44 = f32[1,256,1536]{1,2,0:T(8,128)} copy(f32[1,256,1536]{2,1,0:T(8,128)} %param.13) | data formatting | bytes 3145728 | tf_op args[5]
  35.1 67.3 %all-to-all-done = bf16[8,256,1536]{1,2,0:T(8,128)(2,1)} async-done(((bf16[8,256,1536]{1,2,0:T(8,128)(2,1)}), bf16[8,256,1536]{1,2,0:T(8,128)(2,1)}, u32[]{:S(2)}, u32[]{:S(2)}) %all-to-all-start) | async-done | bytes 6291488 | tf_op jit(solution)/shard_map/all_to_all | solution.py:25
  102.3 3.8 %convert_reduce_fusion = f32[256,1536]{0,1:T(8,128)S(1)} fusion(bf16[8,256,1536]{1,2,0:T(8,128)(2,1)} %all-to-all-done), kind=kLoop, calls=%fused_computation.1 | loop fusion | flops 5898240 | bytes 7864320 | tf_op jit(solution)/shard_map/reduce_sum | solution.py:26
  106.1 1.6 copy.48
  107.8 5.9 %multiply_subtract_fusion = (f32[1,256,1536]{1,2,0:T(8,128)}, f32[1,256,1536]{1,2,0:T(8,128)}, f32[1,256,1536]{1,2,0:T(8,128)}, f32[1,256,1536]{1,2,0:T(8,128)}, f32[1,256,1536]{1,2,0:T(8,128)}) fusion(f32[1,256,1536]{1,2,0:T(8,128)} %copy.46, f32[256,1536]{0,1:T(8,128)S(1)} %convert_reduce_fusion, f32[1,256,1536]{1,2,0:T(8,128)} %copy.41, ...), kind=kLoop, calls=%fused_computation.20 | loop fusion | flops 5898240 | bytes 14155776 | tf_op jit(solution)/shard_map/sub | solution.py:61
  113.6 3.0 %copy.49 = f32[1,256,1536]{2,1,0:T(8,128)} copy(f32[1,256,1536]{1,2,0:T(8,128)} %get-tuple-element.20) | data formatting | bytes 3145728 | tf_op jit(solution)/shard_map/mul | solution.py:58
  116.7 0.0 copy-start.4
  116.7 3.2 %copy.47 = f32[1,256,1536]{2,1,0:T(8,128)} copy(f32[1,256,1536]{1,2,0:T(8,128)} %get-tuple-element.19) | data formatting | bytes 3145728 | tf_op jit(solution)/shard_map/mul | solution.py:57
  119.8 0.0 copy-done.4
  119.8 3.0 %subtract_convert_fusion = bf16[8,2,1,16,1536]{4,3,1,0,2:T(8,128)(2,1)S(1)} fusion(f32[8,2,1,16,1536]{4,3,1,0,2:T(8,128)S(1)} %bitcast.32, f32[8,2,1,16,1536]{4,3,1,0,2:T(8,128)} %bitcast.34, f32[8,2,1,16,1536]{4,3,1,0,2:T(8,128)S(1)} %bitcast.33, f32[8,2,1,16,1536]{4,3,1,0,2:T(8,128)} %bitcast.35), kind=kLoop, calls=%fused_computation.19 | loop fusion | flops 5505024 | bytes 7077888 | tf_op jit(solution)/shard_map/convert_element_type | solution.py:80
  122.8 0.1 copy.50
  122.9 4.4 %all_to_all.27 = bf16[8,2,1,16,1536]{4,3,0,2,1:T(8,128)(2,1)S(1)} all-to-all(bf16[8,2,1,16,1536]{4,3,0,2,1:T(8,128)(2,1)S(1)} %copy.50), channel_id=1, replica_groups=mesh['dp'=8,'expert_0'=4,'expert_1'=2,'expert_2'=2] {'expert_2'}, dimensions={1} | all-to-all | bytes 1572864 | tf_op jit(solution)/shard_map/all_to_all | solution.py:39
  127.3 0.0 copy-start.6
  127.3 0.0 copy-start.7
  127.3 0.9 copy.51
  128.2 4.5 %all-to-all-start.2 = ((bf16[8,2,1,16,1536]{4,3,1,2,0:T(8,128)(2,1)}), bf16[8,2,1,16,1536]{4,3,1,2,0:T(8,128)(2,1)S(1)}, u32[]{:S(2)}, u32[]{:S(2)}) async-start(bf16[8,2,1,16,1536]{4,3,1,2,0:T(8,128)(2,1)} %copy.51), calls=%async_computation.2 | async-start | bytes 1572864 | tf_op jit(solution)/shard_map/all_to_all | solution.py:39
  132.7 0.0 all-gather.2.cloned.1.call-start
  132.7 0.0 copy-done.6
  132.8 0.0 copy-done.7
  132.8 0.1 select_reduce_fusion
  132.9 13.0 %all-to-all-done.2 = bf16[8,2,1,16,1536]{4,3,1,2,0:T(8,128)(2,1)S(1)} async-done(((bf16[8,2,1,16,1536]{4,3,1,2,0:T(8,128)(2,1)}), bf16[8,2,1,16,1536]{4,3,1,2,0:T(8,128)(2,1)S(1)}, u32[]{:S(2)}, u32[]{:S(2)}) %all-to-all-start.2) | async-done | bytes 786464 | tf_op jit(solution)/shard_map/all_to_all | solution.py:39
  145.9 0.6 gather_fusion
  146.5 0.1 broadcast_select_fusion
  146.6 0.0 copy-start.3
  146.7 17.1 %all_to_all.28 = bf16[16,16,1536]{2,1,0:T(8,128)(2,1)} all-to-all(bf16[16,16,1536]{2,1,0:T(8,128)(2,1)S(1)} %broadcast_select_fusion), channel_id=1, replica_groups=mesh['dp'=8,'expert_0'=4,'expert_1'=2,'expert_2'=2] {'expert_0','expert_..., dimensions={0} | all-to-all | bytes 1572864 | tf_op jit(solution)/shard_map/all_to_all | solution.py:83
  163.7 0.0 all-gather.2.cloned.1.call-update
  163.7 0.0 copy-done.3
  163.7 0.0 copy-start.2
  163.8 1.6 copy.52
  165.4 0.0 copy-done.2
  165.4 0.0 copy-start.1
  165.4 1.6 copy.53
  167.0 0.0 copy-done.1
  167.0 1.6 copy.54
  168.6 79.6 %all-gather.2.cloned.1.call-done = bf16[1,2048,1536]{2,1,0:T(8,128)(2,1)} async-done(((bf16[1,256,1536]{2,1,0:T(8,128)(2,1)}), bf16[1,2048,1536]{2,1,0:T(8,128)(2,1)}) %all-gather.2.cloned.1.call-update) | async-done | bytes 6291472 | tf_op jit(solution)/shard_map/all_gather | solution.py:86
  248.2 5.9 %copy.61 = bf16[1,2048,1536]{2,1,0:T(8,128)(2,1)} copy(bf16[1,2048,1536]{2,1,0:T(8,128)(2,1)} %all-gather.2.cloned.1.call-done) | data formatting | bytes 12582912
  (4 shorter events, 0.0 us)
Async XLA Ops:
  20.8 8.0 %copy-start = (f32[1,256,1536]{2,1,0:T(8,128)S(1)}, f32[1,256,1536]{2,1,0:T(8,128)}, u32[]{:S(2)}) copy-start(f32[1,256,1536]{2,1,0:T(8,128)} %param.11) | copy-start | bytes 4718596
  20.8 81.5 %all-to-all-start = ((bf16[8,256,1536]{1,2,0:T(8,128)(2,1)}), bf16[8,256,1536]{1,2,0:T(8,128)(2,1)}, u32[]{:S(2)}, u32[]{:S(2)}) async-start(bf16[8,256,1536]{1,2,0:T(8,128)(2,1)} %bitcast.30), calls=%async_computation | async-start | bytes 12582912 | tf_op jit(solution)/shard_map/all_to_all | solution.py:25
  28.8 1.6 copy-start.5
  116.7 3.2 %copy-start.4 = (f32[256,1536]{1,0:T(8,128)S(1)}, f32[256,1536]{1,0:T(8,128)}, u32[]{:S(2)}) copy-start(f32[256,1536]{1,0:T(8,128)} %copy.48) | copy-start | bytes 4718596
  127.3 5.5 %copy-start.6 = (s32[16]{0:T(128)S(1)}, s32[16]{0:T(128)}, u32[]{:S(2)}) copy-start(s32[16]{0:T(128)} %param.14) | copy-start | bytes 196
  127.3 5.5 %copy-start.7 = (s32[16]{0:T(128)S(1)}, s32[16]{0:T(128)}, u32[]{:S(2)}) copy-start(s32[16]{0:T(128)} %param.15) | copy-start | bytes 196
  128.2 17.7 %all-to-all-start.2 = ((bf16[8,2,1,16,1536]{4,3,1,2,0:T(8,128)(2,1)}), bf16[8,2,1,16,1536]{4,3,1,2,0:T(8,128)(2,1)S(1)}, u32[]{:S(2)}, u32[]{:S(2)}) async-start(bf16[8,2,1,16,1536]{4,3,1,2,0:T(8,128)(2,1)} %copy.51), calls=%async_computation.2 | async-start | bytes 1572864 | tf_op jit(solution)/shard_map/all_to_all | solution.py:39
  132.7 115.5 %all-gather.2.cloned.1.call-start = ((), (), s32[]{:S(2)}) async-start(), calls=%async_computation.4 | async-start | bytes 7077888 | tf_op jit(solution)/shard_map/all_gather | solution.py:86
  146.6 17.1 %copy-start.3 = (f32[1,256,1536]{1,2,0:T(8,128)S(1)}, f32[1,256,1536]{1,2,0:T(8,128)}, u32[]{:S(2)}) copy-start(f32[1,256,1536]{1,2,0:T(8,128)} %get-tuple-element.16) | copy-start | bytes 4718596
  163.7 1.6 copy-start.2
  165.4 1.6 copy-start.1
Sparse Core Ops, SparseCore 0:
  163.9 84.2 all-gather.1
where the time goes:
time: 261 us
  waiting for transfers between devices  160 us (61%)
  local copies, waits for them, and re-layouts  29.5 us (11%)
  blocking collectives  21.4 us (8%)
  between operations  14.8 us (6%)
  other arithmetic  13 us (5%)
  starting transfers between devices  12.6 us (5%)
  matrix products  9.85 us (4%)
    all_gather x1, waiting for transfers between devices, on_device(): moved = lax.all_gather(placed, 'dp', axis=1, tiled=True)  79.6 us
    all_to_all x1, waiting for transfers between devices, sent_and_summed(): lax.all_to_all(blocks, axis, split_axis=0, concat_axis=0, tiled=True)  67.3 us
    all_to_all x1, blocking collectives, on_device(): lax.all_to_all(jnp.take(spread, source, axis=0), EXPERT, split_axis=0, co...  17.1 us
    unnamed x23, local copies, waits for them, and re-layouts  17 us
    all_to_all x1, waiting for transfers between devices, exchange_in_order(): whole = lax.all_to_all(whole, axes[k], k, k, tiled=True)  13 us
    dot_general x1, matrix products, on_device(): lax.dot_general(inputs, cotangent, (((0,), (0,)), ((), ())), preferred_el...  9.85 us
    all_to_all x1, starting transfers between devices, sent_and_summed(): lax.all_to_all(blocks, axis, split_axis=0, concat_axis=0, tiled=True)  8.02 us
    sub x1, other arithmetic, adamw(): master - learn_rate * (first_hat / (jnp.sqrt(second_hat) + adam_eps) + de...  5.87 us
  transfers between devices with their start and end apart: 3, of which 3 were waited for; matrix products, arithmetic and copies ran while one was open for 4% of the time, Pallas kernels for 0%

commit v1 on v0

--- a/solution.py
+++ b/solution.py
@@ -83,7 +83,8 @@
     placed = lax.all_to_all(
         jnp.take(spread, source, axis=0), EXPERT, split_axis=0, concat_axis=1, tiled=True
     )
-    moved = lax.all_gather(placed, "dp", axis=1, tiled=True)
+    stack = jnp.stack([placed] * lax.axis_size("dp"))
+    moved = jnp.concatenate(lax.all_to_all(stack, "dp", 0, 0), axis=1)
     return (updated[None], first[None], second[None], moved)
 
 

time: 261 us -> 244 us (0.935)
  between operations: 14.8 us -> 1.39 us
  waiting for transfers between devices: 160 us -> 149 us
  starting transfers between devices: 12.6 us -> 17.4 us
  local copies, waits for them, and re-layouts: 29.5 us -> 32.7 us
    all_gather x1 -> x0, waiting for transfers between devices: 79.6 us -> none  [on_device(): moved = lax.all_gather(placed, 'dp', axis=1, tiled=True)]
    all_to_all x0 -> x1, waiting for transfers between devices: none -> 68.6 us  [on_device(): moved = jnp.concatenate(lax.all_to_all(stack, 'dp', 0, 0), axis=1)]
    all_to_all x0 -> x1, starting transfers between devices: none -> 4.88 us  [on_device(): moved = jnp.concatenate(lax.all_to_all(stack, 'dp', 0, 0), axis=1)]
    another operation x0 -> x1, local copies, waits for them, and re-layouts: none -> 3.24 us  [on_device(): stack = jnp.stack([placed] * lax.axis_size('dp'))]
  transfers between devices with their start and end apart: 3 -> 3, of which waited for: 3 -> 3; matrix products, arithmetic and copies ran while one was open for 4% -> 5% of each run, Pallas kernels for 0% -> 0%
where the time goes in v1:
time: 244 us
  waiting for transfers between devices  149 us (61%)
  local copies, waits for them, and re-layouts  32.7 us (13%)
  blocking collectives  20.6 us (8%)
  starting transfers between devices  17.4 us (7%)
  other arithmetic  13 us (5%)
  matrix products  9.85 us (4%)
    all_to_all x1, waiting for transfers between devices, on_device(): moved = jnp.concatenate(lax.all_to_all(stack, 'dp', 0, 0), axis=1)  68.6 us
    all_to_all x1, waiting for transfers between devices, sent_and_summed(): lax.all_to_all(blocks, axis, split_axis=0, concat_axis=0, tiled=True)  67.3 us
    unnamed x23, local copies, waits for them, and re-layouts  17 us
    all_to_all x1, blocking collectives, on_device(): lax.all_to_all(jnp.take(spread, source, axis=0), EXPERT, split_axis=0, co...  16.3 us
    all_to_all x1, waiting for transfers between devices, exchange_in_order(): whole = lax.all_to_all(whole, axes[k], k, k, tiled=True)  13 us
    dot_general x1, matrix products, on_device(): lax.dot_general(inputs, cotangent, (((0,), (0,)), ((), ())), preferred_el...  9.85 us
    all_to_all x1, starting transfers between devices, sent_and_summed(): lax.all_to_all(blocks, axis, split_axis=0, concat_axis=0, tiled=True)  8.02 us
    sub x1, other arithmetic, adamw(): master - learn_rate * (first_hat / (jnp.sqrt(second_hat) + adam_eps) + de...  5.87 us
  transfers between devices with their start and end apart: 3, of which 3 were waited for; matrix products, arithmetic and copies ran while one was open for 5% of the time, Pallas kernels for 0%

profile of v1, /device:TPU:0, one launch (start us, length us, event | category | flops | bytes accessed | tf_op | source)
XLA Modules:
  0.0 243.8 jit_solution(12401348100046426274)
XLA Ops:
  1.3 9.9 %multiply_convert_fusion = bf16[1536,2048]{1,0:T(8,128)(2,1)S(1)} fusion(bf16[1,1024,2048]{2,1,0:T(8,128)(2,1)} %param.8, bf16[1,1024,1536]{2,1,0:T(8,128)(2,1)} %param.9, pred[1024]{0:T(1024)(128)(4,1)S(1)} %iota_compare_fusion.1), kind=kOutput, calls=%fused_computation.2 | convolution fusion | flops 6450315264 | bytes 13632512 | tf_op jit(solution)/shard_map/dot_general | solution.py:75
  11.1 3.1 %copy.58 = bf16[192,8,8,256]{3,2,0,1:T(8,128)(2,1)} copy(bf16[192,8,8,256]{3,2,1,0:T(8,128)(2,1)S(1)} %bitcast.32) | data formatting | bytes 12582912 | tf_op jit(solution)/shard_map/reshape | solution.py:19
  14.3 0.0 copy-start
  14.3 8.0 %all-to-all-start = ((bf16[8,256,1536]{1,2,0:T(8,128)(2,1)}), bf16[8,256,1536]{1,2,0:T(8,128)(2,1)}, u32[]{:S(2)}, u32[]{:S(2)}) async-start(bf16[8,256,1536]{1,2,0:T(8,128)(2,1)} %bitcast.31), calls=%async_computation | async-start | bytes 12582912 | tf_op jit(solution)/shard_map/all_to_all | solution.py:25
  22.3 0.0 copy-done
  22.3 0.0 copy-start.5
  22.3 1.6 copy.46
  23.9 0.0 copy-done.5
  23.9 1.6 copy.41
  25.5 3.0 %copy.44 = f32[1,256,1536]{1,2,0:T(8,128)} copy(f32[1,256,1536]{2,1,0:T(8,128)} %param.13) | data formatting | bytes 3145728 | tf_op args[5]
  28.5 67.3 %all-to-all-done = bf16[8,256,1536]{1,2,0:T(8,128)(2,1)} async-done(((bf16[8,256,1536]{1,2,0:T(8,128)(2,1)}), bf16[8,256,1536]{1,2,0:T(8,128)(2,1)}, u32[]{:S(2)}, u32[]{:S(2)}) %all-to-all-start) | async-done | bytes 6291488 | tf_op jit(solution)/shard_map/all_to_all | solution.py:25
  95.8 3.8 %convert_reduce_fusion = f32[256,1536]{0,1:T(8,128)S(1)} fusion(bf16[8,256,1536]{1,2,0:T(8,128)(2,1)} %all-to-all-done), kind=kLoop, calls=%fused_computation.1 | loop fusion | flops 5898240 | bytes 7864320 | tf_op jit(solution)/shard_map/reduce_sum | solution.py:26
  99.6 1.6 copy.48
  101.2 5.9 %multiply_subtract_fusion = (f32[1,256,1536]{1,2,0:T(8,128)}, f32[1,256,1536]{1,2,0:T(8,128)}, f32[1,256,1536]{1,2,0:T(8,128)}, f32[1,256,1536]{1,2,0:T(8,128)}, f32[1,256,1536]{1,2,0:T(8,128)}) fusion(f32[1,256,1536]{1,2,0:T(8,128)} %copy.46, f32[256,1536]{0,1:T(8,128)S(1)} %convert_reduce_fusion, f32[1,256,1536]{1,2,0:T(8,128)} %copy.41, ...), kind=kLoop, calls=%fused_computation.20 | loop fusion | flops 5898240 | bytes 14155776 | tf_op jit(solution)/shard_map/sub | solution.py:61
  107.1 3.0 %copy.49 = f32[1,256,1536]{2,1,0:T(8,128)} copy(f32[1,256,1536]{1,2,0:T(8,128)} %get-tuple-element.20) | data formatting | bytes 3145728 | tf_op jit(solution)/shard_map/mul | solution.py:58
  110.1 0.0 copy-start.4
  110.1 3.1 %copy.47 = f32[1,256,1536]{2,1,0:T(8,128)} copy(f32[1,256,1536]{1,2,0:T(8,128)} %get-tuple-element.19) | data formatting | bytes 3145728 | tf_op jit(solution)/shard_map/mul | solution.py:57
  113.3 0.0 copy-done.4
  113.3 3.0 %subtract_convert_fusion = bf16[8,2,1,16,1536]{4,3,1,0,2:T(8,128)(2,1)S(1)} fusion(f32[8,2,1,16,1536]{4,3,1,0,2:T(8,128)S(1)} %bitcast.33, f32[8,2,1,16,1536]{4,3,1,0,2:T(8,128)} %bitcast.35, f32[8,2,1,16,1536]{4,3,1,0,2:T(8,128)S(1)} %bitcast.34, f32[8,2,1,16,1536]{4,3,1,0,2:T(8,128)} %bitcast.36), kind=kLoop, calls=%fused_computation.19 | loop fusion | flops 5505024 | bytes 7077888 | tf_op jit(solution)/shard_map/convert_element_type | solution.py:80
  116.3 0.1 copy.50
  116.3 4.4 %all_to_all.29 = bf16[8,2,1,16,1536]{4,3,0,2,1:T(8,128)(2,1)S(1)} all-to-all(bf16[8,2,1,16,1536]{4,3,0,2,1:T(8,128)(2,1)S(1)} %copy.50), channel_id=1, replica_groups=mesh['dp'=8,'expert_0'=4,'expert_1'=2,'expert_2'=2] {'expert_2'}, dimensions={1} | all-to-all | bytes 1572864 | tf_op jit(solution)/shard_map/all_to_all | solution.py:39
  120.7 0.0 copy-start.6
  120.7 0.0 copy-start.7
  120.7 0.9 copy.51
  121.6 4.5 %all-to-all-start.2 = ((bf16[8,2,1,16,1536]{4,3,1,2,0:T(8,128)(2,1)}), bf16[8,2,1,16,1536]{4,3,1,2,0:T(8,128)(2,1)S(1)}, u32[]{:S(2)}, u32[]{:S(2)}) async-start(bf16[8,2,1,16,1536]{4,3,1,2,0:T(8,128)(2,1)} %copy.51), calls=%async_computation.2 | async-start | bytes 1572864 | tf_op jit(solution)/shard_map/all_to_all | solution.py:39
  126.1 0.0 copy-done.6
  126.1 0.0 copy-done.7
  126.1 0.1 select_reduce_fusion
  126.3 13.0 %all-to-all-done.2 = bf16[8,2,1,16,1536]{4,3,1,2,0:T(8,128)(2,1)S(1)} async-done(((bf16[8,2,1,16,1536]{4,3,1,2,0:T(8,128)(2,1)}), bf16[8,2,1,16,1536]{4,3,1,2,0:T(8,128)(2,1)S(1)}, u32[]{:S(2)}, u32[]{:S(2)}) %all-to-all-start.2) | async-done | bytes 786464 | tf_op jit(solution)/shard_map/all_to_all | solution.py:39
  139.3 0.6 gather_fusion
  139.9 0.1 broadcast_select_fusion
  140.1 16.3 %all_to_all.30 = bf16[16,16,1536]{2,1,0:T(8,128)(2,1)S(1)} all-to-all(bf16[16,16,1536]{2,1,0:T(8,128)(2,1)S(1)} %broadcast_select_fusion), channel_id=1, replica_groups=mesh['dp'=8,'expert_0'=4,'expert_1'=2,'expert_2'=2] {'expert_0','expert_..., dimensions={0} | all-to-all | bytes 1572864 | tf_op jit(solution)/shard_map/all_to_all | solution.py:83
  156.4 3.2 %stack.5 = bf16[8,1,256,1536]{3,2,1,0:T(8,128)(2,1)} broadcast(bf16[256,1536]{1,0:T(8,128)(2,1)S(1)} %bitcast.37), dimensions={2,3} | broadcast | bytes 7077888 | tf_op jit(solution)/shard_map/stack | solution.py:86
  159.6 0.0 copy-start.3
  159.6 4.9 %all-to-all-start.4 = ((bf16[8,1,256,1536]{3,2,1,0:T(8,128)(2,1)}), bf16[8,1,256,1536]{3,2,1,0:T(8,128)(2,1)}, u32[]{:S(2)}, u32[]{:S(2)}) async-start(bf16[8,1,256,1536]{3,2,1,0:T(8,128)(2,1)} %stack.5), calls=%async_computation.4 | async-start | bytes 12582912 | tf_op jit(solution)/shard_map/all_to_all | solution.py:87
  164.5 0.0 copy-done.3
  164.5 0.0 copy-start.2
  164.5 1.6 copy.52
  166.1 0.0 copy-done.2
  166.1 0.0 copy-start.1
  166.1 1.6 copy.53
  167.7 0.0 copy-done.1
  167.7 1.6 copy.54
  169.3 68.6 %all-to-all-done.4 = bf16[8,1,256,1536]{3,2,1,0:T(8,128)(2,1)} async-done(((bf16[8,1,256,1536]{3,2,1,0:T(8,128)(2,1)}), bf16[8,1,256,1536]{3,2,1,0:T(8,128)(2,1)}, u32[]{:S(2)}, u32[]{:S(2)}) %all-to-all-start.4) | async-done | bytes 6291488 | tf_op jit(solution)/shard_map/all_to_all | solution.py:87
  237.9 5.9 %copy.61 = bf16[1,2048,1536]{2,1,0:T(8,128)(2,1)} copy(bf16[1,2048,1536]{2,1,0:T(8,128)(2,1)} %bitcast.13) | data formatting | bytes 12582912
  (4 shorter events, 0.0 us)
Async XLA Ops:
  14.3 8.0 %copy-start = (f32[1,256,1536]{2,1,0:T(8,128)S(1)}, f32[1,256,1536]{2,1,0:T(8,128)}, u32[]{:S(2)}) copy-start(f32[1,256,1536]{2,1,0:T(8,128)} %param.11) | copy-start | bytes 4718596
  14.3 81.5 %all-to-all-start = ((bf16[8,256,1536]{1,2,0:T(8,128)(2,1)}), bf16[8,256,1536]{1,2,0:T(8,128)(2,1)}, u32[]{:S(2)}, u32[]{:S(2)}) async-start(bf16[8,256,1536]{1,2,0:T(8,128)(2,1)} %bitcast.31), calls=%async_computation | async-start | bytes 12582912 | tf_op jit(solution)/shard_map/all_to_all | solution.py:25
  22.3 1.6 copy-start.5
  110.1 3.1 %copy-start.4 = (f32[256,1536]{1,0:T(8,128)S(1)}, f32[256,1536]{1,0:T(8,128)}, u32[]{:S(2)}) copy-start(f32[256,1536]{1,0:T(8,128)} %copy.48) | copy-start | bytes 4718596
  120.7 5.4 %copy-start.6 = (s32[16]{0:T(128)S(1)}, s32[16]{0:T(128)}, u32[]{:S(2)}) copy-start(s32[16]{0:T(128)} %param.14) | copy-start | bytes 196
  120.7 5.4 %copy-start.7 = (s32[16]{0:T(128)S(1)}, s32[16]{0:T(128)}, u32[]{:S(2)}) copy-start(s32[16]{0:T(128)} %param.15) | copy-start | bytes 196
  121.6 17.7 %all-to-all-start.2 = ((bf16[8,2,1,16,1536]{4,3,1,2,0:T(8,128)(2,1)}), bf16[8,2,1,16,1536]{4,3,1,2,0:T(8,128)(2,1)S(1)}, u32[]{:S(2)}, u32[]{:S(2)}) async-start(bf16[8,2,1,16,1536]{4,3,1,2,0:T(8,128)(2,1)} %copy.51), calls=%async_computation.2 | async-start | bytes 1572864 | tf_op jit(solution)/shard_map/all_to_all | solution.py:39
  159.6 4.9 %copy-start.3 = (f32[1,256,1536]{1,2,0:T(8,128)S(1)}, f32[1,256,1536]{1,2,0:T(8,128)}, u32[]{:S(2)}) copy-start(f32[1,256,1536]{1,2,0:T(8,128)} %get-tuple-element.16) | copy-start | bytes 4718596
  159.6 78.4 %all-to-all-start.4 = ((bf16[8,1,256,1536]{3,2,1,0:T(8,128)(2,1)}), bf16[8,1,256,1536]{3,2,1,0:T(8,128)(2,1)}, u32[]{:S(2)}, u32[]{:S(2)}) async-start(bf16[8,1,256,1536]{3,2,1,0:T(8,128)(2,1)} %stack.5), calls=%async_computation.4 | async-start | bytes 12582912 | tf_op jit(solution)/shard_map/all_to_all | solution.py:87
  164.5 1.6 copy-start.2
  166.1 1.6 copy-start.1
